TPU v7x, 512 devices: a whole 4x8x8 slice. The times are simulated.
512 devices in a mesh: tor: 8 (over z_lo, x), pol: 64 (over y, z_hi, core).
Axes of the slice: x: 4, y: 8, z: 8 (z_hi: 4, z_lo: 2; z = z_hi * 2 + z_lo), core: 2. Of those that a mesh axis runs over, the one named last changes fastest.
Arguments:
- plasma_state: float32 [6, 8, 512, 256], P(None, 'tor', 'pol'), may hold values from -3 to 3
- right_side: float32 [6, 8, 512, 256], P(None, 'tor', 'pol'), may hold values from -12 to 12
- resistivity: float32 [8, 512, 256], P('tor', 'pol'), may hold values from 0.05 to 0.6
- jacobi_blocks: float32 [6, 6, 8, 512, 256], P(None, None, 'tor', 'pol'), may hold values from -0.6 to 1.6, as said below
Outputs:
- update: float32 [6, 8, 512, 256], P(None, 'tor', 'pol')
- estimates: float32 [3], replicated
Inputs may be any that keep to these rules, and one draw needn't show every extreme that they name: `jacobi_blocks`: each block's diagonal entries lie in 0.4 to 1.6.
All inputs are finite; a program needn't handle non-finite values.
Results may differ from a plain program's by a relative error of at most 0.006.
Values may be sent and summed in bfloat16 or wider, within the bound.
A program may use at most 64 MiB of HBM per device.

v0:
```python
import jax
import jax.numpy as jnp
from jax import lax
from jax.sharding import PartitionSpec as P

ITERS = 3
inverse_step = 1.0
viscosity = 0.2
epsilon = 1e-06


def padded_2(cells, sides, width, closed):
    for axis, dim in sides:
        count = lax.axis_size(axis)
        ends = count if closed else count - 1
        head = lax.slice_in_dim(cells, 0, width, axis=dim)
        tail = lax.slice_in_dim(cells, cells.shape[dim] - width, cells.shape[dim], axis=dim)
        cells = jnp.concatenate(
            [
                lax.ppermute(tail, axis, [(i, (i + 1) % count) for i in range(ends)]),
                cells,
                lax.ppermute(head, axis, [((i + 1) % count, i) for i in range(ends)]),
            ],
            axis=dim,
        )
    return cells


def neighbour(values, array_axis, offset):
    length = values.shape[array_axis]
    widths = [(0, 0)] * values.ndim
    widths[array_axis] = (1, 1)
    padded = jnp.pad(values, widths)
    return lax.slice_in_dim(padded, 1 + offset, 1 + offset + length, axis=array_axis)


def linear_flux(plasma, tangent, direction):
    magnetic = plasma[0:3]
    velocity = plasma[3:6]
    tang_mag = tangent[0:3]
    tang_vel = tangent[3:6]
    pressure = jnp.sum(magnetic * tang_mag, axis=0)
    components = []
    for inner_index in range(3):
        components.append(
            tang_vel[direction] * magnetic[inner_index]
            + velocity[direction] * tang_mag[inner_index]
            - tang_mag[direction] * velocity[inner_index]
            - magnetic[direction] * tang_vel[inner_index]
        )
    for inner_index in range(3):
        moment = (
            tang_vel[direction] * velocity[inner_index]
            + velocity[direction] * tang_vel[inner_index]
            - tang_mag[direction] * magnetic[inner_index]
            - magnetic[direction] * tang_mag[inner_index]
        )
        if inner_index == direction:
            moment = moment + pressure
        components.append(moment)
    return jnp.stack(components)


def diffusion_field(resistivity):
    shape = (3,) + resistivity.shape
    return jnp.concatenate(
        [jnp.broadcast_to(resistivity[None], shape), jnp.full(shape, viscosity, jnp.float32)]
    )


def jacobian_product(
    plasma, tangent, plasma_planes, tangent_planes, plasma_rows, tangent_rows, diffusion
):
    result_sum = inverse_step * tangent
    flux_planes = linear_flux(plasma_planes, tangent_planes, 0)
    result_sum = result_sum + 0.5 * (flux_planes[:, 2:] - flux_planes[:, :-2])
    laplace_sum = tangent_planes[:, 2:] + tangent_planes[:, :-2] - 2.0 * tangent
    flux_rows = linear_flux(plasma_rows, tangent_rows, 1)
    result_sum = result_sum + 0.5 * (flux_rows[:, :, 2:] - flux_rows[:, :, :-2])
    laplace_sum = laplace_sum + tangent_rows[:, :, 2:] + tangent_rows[:, :, :-2] - 2.0 * tangent
    flux_depth = linear_flux(plasma, tangent, 2)
    result_sum = result_sum + 0.5 * (neighbour(flux_depth, 3, 1) - neighbour(flux_depth, 3, -1))
    laplace_sum = laplace_sum + neighbour(tangent, 3, 1) + neighbour(tangent, 3, -1) - 2.0 * tangent
    return result_sum - diffusion * laplace_sum


def precondition(blocks, vector):
    widened = vector.astype(jnp.float32)
    total = blocks[:, 0] * widened[0]
    for column in range(1, 6):
        total = total + blocks[:, column] * widened[column]
    return total


def least_squares(columns, initial_norm):
    count = len(columns)
    rhs_list = [initial_norm] + [jnp.float32(0.0)] * count
    cosines = []
    sines = []
    triangle = []
    estimate_list = []
    for column in range(count):
        entries = list(columns[column])
        for inner_index in range(column):
            first_value = entries[inner_index]
            second_value = entries[inner_index + 1]
            entries[inner_index] = (
                cosines[inner_index] * first_value + sines[inner_index] * second_value
            )
            entries[inner_index + 1] = (
                -sines[inner_index] * first_value + cosines[inner_index] * second_value
            )
        first_value = entries[column]
        second_value = entries[column + 1]
        radius = jnp.sqrt(first_value * first_value + second_value * second_value)
        cosine = first_value / radius
        sine_value = second_value / radius
        cosines.append(cosine)
        sines.append(sine_value)
        entries[column] = radius
        triangle.append(entries[: column + 1])
        previous = rhs_list[column]
        rhs_list[column] = cosine * previous
        rhs_list[column + 1] = -sine_value * previous
        estimate_list.append(jnp.abs(rhs_list[column + 1]))
    weights = [jnp.float32(0.0)] * count
    for column in reversed(range(count)):
        partial_value = rhs_list[column]
        for later in range(column + 1, count):
            partial_value = partial_value - triangle[later][column] * weights[later]
        weights[column] = partial_value / triangle[column][column]
    return (weights, estimate_list)


def shards(plasma_state, right_side, resistivity, jacobi_blocks):
    cell_count = (
        6
        * plasma_state.shape[1]
        * plasma_state.shape[2]
        * plasma_state.shape[3]
        * lax.axis_size("tor")
        * lax.axis_size("pol")
    )
    diffusion = diffusion_field(resistivity)
    plasma_planes = padded_2(plasma_state.astype(jnp.bfloat16), (("tor", 1),), 1, True).astype(
        plasma_state.dtype
    )
    plasma_rows = padded_2(plasma_state, (("pol", 2),), 1, False)
    square_sum = lax.psum(jnp.sum(right_side * right_side), ("tor", "pol"))
    initial_norm = jnp.sqrt(square_sum + epsilon)
    krylov_basis = [(right_side / initial_norm).astype(jnp.bfloat16)]
    directions = []
    columns = []
    for column in range(ITERS):
        vector = krylov_basis[column]
        tangent = precondition(jacobi_blocks, vector)
        tangent_planes = padded_2(tangent.astype(jnp.bfloat16), (("tor", 1),), 1, True).astype(
            tangent.dtype
        )
        tangent_rows = padded_2(tangent, (("pol", 2),), 1, False)
        image = jacobian_product(
            plasma_state,
            tangent,
            plasma_planes,
            tangent_planes,
            plasma_rows,
            tangent_rows,
            diffusion,
        )
        directions.append(tangent)
        local_products = jnp.stack(
            [jnp.sum(image * earlier.astype(jnp.float32)) for earlier in krylov_basis]
        )
        products = lax.psum(local_products, ("tor", "pol"))
        coefficients = [products[inner_index] for inner_index in range(column + 1)]
        remainder = image
        for inner_index in range(column + 1):
            remainder = remainder - coefficients[inner_index] * krylov_basis[inner_index].astype(
                jnp.float32
            )
        remainder_square = lax.psum(jnp.sum(remainder * remainder), ("tor", "pol"))
        new_norm = jnp.sqrt(remainder_square + epsilon)
        columns.append(coefficients + [new_norm])
        if column + 1 < ITERS:
            krylov_basis.append((remainder / new_norm).astype(jnp.bfloat16))
    weights, estimate_list = least_squares(columns, initial_norm)
    update = weights[0] * directions[0]
    for column in range(1, ITERS):
        update = update + weights[column] * directions[column]
    estimates = jnp.stack(estimate_list) / jnp.sqrt(jnp.float32(cell_count))
    return (update, estimates)


def solution(mesh):
    return jax.shard_map(
        shards,
        mesh=mesh,
        in_specs=(
            P(None, "tor", "pol", None),
            P(None, "tor", "pol", None),
            P("tor", "pol", None),
            P(None, None, "tor", "pol", None),
        ),
        out_specs=(P(None, "tor", "pol", None), P()),
        check_vma=False,
    )
```

profile of v0, /device:TPU:1, one launch (start us, length us, event | category | flops | bytes accessed | tf_op | source)
XLA Modules:
  0.0 785.8 jit_solution(5154822776508504955)
XLA Ops:
  0.6 1.5 multiply_reduce_fusion.5
  2.1 106.1 %psum.49 = f32[]{:T(128)} all-reduce(f32[]{:T(128)} %multiply_reduce_fusion.5), channel_id=1, replica_groups=mesh['tor'=8,'pol'=64] {'tor','pol'}, use_global_device_ids=true, to_apply=%region_1.0 | all-reduce | flops 1 | bytes 8 | tf_op jit(solution)/shard_map/psum | solution.py:149
  109.9 2.5 collective-permute-start
  112.4 4.9 collective-permute-start.1
  117.3 1.9 collective-permute-start.2
  119.3 3.0 collective-permute-start.4
  122.3 1.9 collective-permute-start.5
  124.3 4.5 collective-permute-start.6
  128.9 1.9 collective-permute-start.7
  130.9 5.8 collective-permute-start.3
  139.1 104.8 %psum.50 = f32[]{:T(128)} all-reduce(f32[]{:T(128)} %get-tuple-element.15), channel_id=1, replica_groups=mesh['tor'=8,'pol'=64] {'tor','pol'}, use_global_device_ids=true, to_apply=%region_6.7 | all-reduce | flops 1 | bytes 8 | tf_op jit(solution)/shard_map/psum | solution.py:174
  243.9 1.3 multiply_reduce_fusion.4
  245.2 95.1 %psum.51 = f32[]{:T(128)} all-reduce(f32[]{:T(128)} %multiply_reduce_fusion.4), channel_id=1, replica_groups=mesh['tor'=8,'pol'=64] {'tor','pol'}, use_global_device_ids=true, to_apply=%region_8.9 | all-reduce | flops 1 | bytes 8 | tf_op jit(solution)/shard_map/psum | solution.py:181
  341.7 3.7 collective-permute-start.8
  345.4 3.7 collective-permute-start.9
  349.2 3.1 collective-permute-start.10
  352.3 1.9 collective-permute-start.11
  356.3 1.8 collective-permute-done.11
  359.2 1.4 pad_maximum_fusion.10
  360.6 101.5 %psum.52 = f32[2]{0:T(128)S(1)} all-reduce(f32[2]{0:T(128)S(1)} %pad_maximum_fusion.10), channel_id=1, replica_groups=mesh['tor'=8,'pol'=64] {'tor','pol'}, use_global_device_ids=true, to_apply=%region_14.15 | all-reduce | flops 2 | bytes 16 | tf_op jit(solution)/shard_map/psum | solution.py:174
  462.7 1.9 multiply_reduce_fusion.2
  464.6 95.6 %psum.53 = f32[]{:T(128)} all-reduce(f32[]{:T(128)} %multiply_reduce_fusion.2), channel_id=1, replica_groups=mesh['tor'=8,'pol'=64] {'tor','pol'}, use_global_device_ids=true, to_apply=%region_16.17 | all-reduce | flops 1 | bytes 8 | tf_op jit(solution)/shard_map/psum | solution.py:181
  560.8 1.3 fusion.80
  562.2 2.8 collective-permute-start.12
  565.0 4.6 collective-permute-start.13
  569.6 3.0 collective-permute-start.14
  572.6 1.9 collective-permute-start.15
  577.4 1.1 collective-permute-done.15
  579.6 2.0 pad_maximum_fusion.11
  581.6 99.6 %psum.54 = f32[3]{0:T(128)S(1)} all-reduce(f32[3]{0:T(128)S(1)} %pad_maximum_fusion.11), channel_id=1, replica_groups=mesh['tor'=8,'pol'=64] {'tor','pol'}, use_global_device_ids=true, to_apply=%region_23.24 | all-reduce | flops 3 | bytes 24 | tf_op jit(solution)/shard_map/psum | solution.py:174
  684.4 2.6 fusion.13
  687.6 95.3 %psum.55 = f32[]{:T(128)} all-reduce(f32[]{:T(128)} %fusion.13), channel_id=1, replica_groups=mesh['tor'=8,'pol'=64] {'tor','pol'}, use_global_device_ids=true, to_apply=%region_25.26 | all-reduce | flops 1 | bytes 8 | tf_op jit(solution)/shard_map/psum | solution.py:181
  (114 shorter events, 8.7 us)
Async XLA Ops:
  0.6 108.3 %copy-start.2 = (f32[6,1,8,256]{3,2,1,0:T(8,128)S(1)}, f32[6,1,8,256]{3,2,1,0:T(8,128)}, u32[]{:S(2)}) copy-start(f32[6,1,8,256]{3,2,1,0:T(8,128)} %param.5) | copy-start | bytes 147460
  108.9 8.4 %copy-start = (f32[6,1,8,256]{3,2,1,0:T(8,128)S(1)}, f32[6,1,8,256]{3,2,1,0:T(8,128)}, u32[]{:S(2)}) copy-start(f32[6,1,8,256]{3,2,1,0:T(8,128)} %param.4) | copy-start | bytes 147460
  109.9 26.9 %collective-permute-start = (bf16[6,1,8,256]{3,2,1,0:T(8,128)(2,1)S(1)}, bf16[6,1,8,256]{3,2,1,0:T(8,128)(2,1)S(1)}, u32[]{:S(2)}, u32[]{:S(2)}) collective-permute-start(bf16[6,1,8,256]{3,2,1,0:T(8,128)(2,1)S(1)} %get-tuple-element.17), channel_id=1, source_target_pairs={{0,64},{64,128},{128,192},{192,256},{256,320},{320,384},{384,448},... | collective-permute-start | bytes 73736 | tf_op jit(solution)/shard_map/ppermute | solution.py:20
  112.4 24.4 %collective-permute-start.1 = (bf16[6,1,8,256]{3,2,1,0:T(8,128)(2,1)S(1)}, bf16[6,1,8,256]{3,2,1,0:T(8,128)(2,1)S(1)}, u32[]{:S(2)}, u32[]{:S(2)}) collective-permute-start(bf16[6,1,8,256]{3,2,1,0:T(8,128)(2,1)S(1)} %get-tuple-element.17), channel_id=1, source_target_pairs={{64,0},{128,64},{192,128},{256,192},{320,256},{384,320},{448,384},... | collective-permute-start | bytes 73736 | tf_op jit(solution)/shard_map/ppermute | solution.py:22
  117.3 19.5 %collective-permute-start.2 = (bf16[6,1,8,256]{3,2,1,0:T(8,128)(2,1)S(1)}, bf16[6,1,8,256]{3,2,1,0:T(8,128)(2,1)S(1)}, u32[]{:S(2)}, u32[]{:S(2)}) collective-permute-start(bf16[6,1,8,256]{3,2,1,0:T(8,128)(2,1)S(1)} %convert_element_type.95), channel_id=1, source_target_pairs={{0,64},{64,128},{128,192},{192,256},{256,320},{320,384},{384,448},... | collective-permute-start | bytes 73736 | tf_op jit(solution)/shard_map/ppermute | solution.py:20
  119.3 5.1 collective-permute-start.4
  122.3 6.6 collective-permute-start.5
  124.3 6.5 collective-permute-start.6
  128.9 7.7 collective-permute-start.7
  130.9 6.7 collective-permute-start.3
  137.7 0.7 copy-start.3
  139.1 202.6 %copy-start.1 = (f32[6,6,1,8,256]{4,3,2,1,0:T(8,128)S(1)}, f32[6,6,1,8,256]{4,3,2,1,0:T(8,128)}, u32[]{:S(2)}) copy-start(f32[6,6,1,8,256]{4,3,2,1,0:T(8,128)} %param.7) | copy-start | bytes 884740
  341.7 16.6 %collective-permute-start.8 = (bf16[6,1,8,256]{3,2,1,0:T(8,128)(2,1)S(1)}, bf16[6,1,8,256]{3,2,1,0:T(8,128)(2,1)S(1)}, u32[]{:S(2)}, u32[]{:S(2)}) collective-permute-start(bf16[6,1,8,256]{3,2,1,0:T(8,128)(2,1)S(1)} %get-tuple-element.11), channel_id=1, source_target_pairs={{0,64},{64,128},{128,192},{192,256},{256,320},{320,384},{384,448},... | collective-permute-start | bytes 73736 | tf_op jit(solution)/shard_map/ppermute | solution.py:20
  345.4 12.9 %collective-permute-start.9 = (bf16[6,1,8,256]{3,2,1,0:T(8,128)(2,1)S(1)}, bf16[6,1,8,256]{3,2,1,0:T(8,128)(2,1)S(1)}, u32[]{:S(2)}, u32[]{:S(2)}) collective-permute-start(bf16[6,1,8,256]{3,2,1,0:T(8,128)(2,1)S(1)} %get-tuple-element.11), channel_id=1, source_target_pairs={{64,0},{128,64},{192,128},{256,192},{320,256},{384,320},{448,384},... | collective-permute-start | bytes 73736 | tf_op jit(solution)/shard_map/ppermute | solution.py:22
  349.2 7.2 collective-permute-start.10
  352.3 5.8 collective-permute-start.11
  562.2 16.5 %collective-permute-start.12 = (bf16[6,1,8,256]{3,2,1,0:T(8,128)(2,1)S(1)}, bf16[6,1,8,256]{3,2,1,0:T(8,128)(2,1)S(1)}, u32[]{:S(2)}, u32[]{:S(2)}) collective-permute-start(bf16[6,1,8,256]{3,2,1,0:T(8,128)(2,1)S(1)} %get-tuple-element.8), channel_id=1, source_target_pairs={{0,64},{64,128},{128,192},{192,256},{256,320},{320,384},{384,448},... | collective-permute-start | bytes 73736 | tf_op jit(solution)/shard_map/ppermute | solution.py:20
  565.0 13.7 %collective-permute-start.13 = (bf16[6,1,8,256]{3,2,1,0:T(8,128)(2,1)S(1)}, bf16[6,1,8,256]{3,2,1,0:T(8,128)(2,1)S(1)}, u32[]{:S(2)}, u32[]{:S(2)}) collective-permute-start(bf16[6,1,8,256]{3,2,1,0:T(8,128)(2,1)S(1)} %get-tuple-element.8), channel_id=1, source_target_pairs={{64,0},{128,64},{192,128},{256,192},{320,256},{384,320},{448,384},... | collective-permute-start | bytes 73736 | tf_op jit(solution)/shard_map/ppermute | solution.py:22
  569.6 7.7 collective-permute-start.14
  572.6 5.8 collective-permute-start.15
where the time goes:
time: 787 us; the launch traced here: 786 us
  blocking collectives  698 us (89%)
  starting transfers between devices  51.1 us (6%)
  other arithmetic  18 us (2%)
  between operations  13.1 us (2%)
    psum x3, blocking collectives, shards(): products = lax.psum(local_products, ('tor', 'pol'))  306 us
    psum x3, blocking collectives, shards(): remainder_square = lax.psum(jnp.sum(remainder * remainder), ('tor', 'pol'))  286 us
    psum x1, blocking collectives, shards(): square_sum = lax.psum(jnp.sum(right_side * right_side), ('tor', 'pol'))  106 us
    ppermute x8, starting transfers between devices, padded_2(): lax.ppermute(head, axis, [((i + 1) % count, i) for i in range(ends)])  26.7 us
    ppermute x8, starting transfers between devices, padded_2(): lax.ppermute(tail, axis, [(i, (i + 1) % count) for i in range(ends)])  24.5 us
  transfers between devices with their start and end apart: 16, of which 3 were waited for; matrix products, arithmetic and copies ran while one was open for 0% of the time, Pallas kernels for 0%

commit v1 on v0

--- a/solution.py
+++ b/solution.py
@@ -171,7 +171,8 @@
         local_products = jnp.stack(
             [jnp.sum(image * earlier.astype(jnp.float32)) for earlier in krylov_basis]
         )
-        products = lax.psum(local_products, ("tor", "pol"))
+        one_axis = lax.psum(local_products, "pol")
+        products = lax.psum(one_axis, "tor")
         coefficients = [products[inner_index] for inner_index in range(column + 1)]
         remainder = image
         for inner_index in range(column + 1):

time: 787 us -> 973 us (1.24)
  blocking collectives: 698 us -> 881 us
    psum x3 -> x6, blocking collectives: 306 us -> 452 us  [the longest x3 410 us: shards(): one_axis = lax.psum(local_products, 'pol')]
    psum x3, blocking collectives: 286 us -> 323 us  [shards(): remainder_square = lax.psum(jnp.sum(remainder * remainder), ('tor', 'pol'))]
where the time goes in v1:
time: 973 us; the launch traced here: 971 us
  blocking collectives  881 us (91%)
  starting transfers between devices  53.3 us (5%)
  other arithmetic  18 us (2%)
  between operations  13.1 us (1%)
    psum x3, blocking collectives, shards(): one_axis = lax.psum(local_products, 'pol')  410 us
    psum x3, blocking collectives, shards(): remainder_square = lax.psum(jnp.sum(remainder * remainder), ('tor', 'pol'))  323 us
    psum x1, blocking collectives, shards(): square_sum = lax.psum(jnp.sum(right_side * right_side), ('tor', 'pol'))  106 us
    psum x3, blocking collectives, shards(): products = lax.psum(one_axis, 'tor')  42.2 us
    ppermute x8, starting transfers between devices, padded_2(): lax.ppermute(tail, axis, [(i, (i + 1) % count) for i in range(ends)])  27.3 us
    ppermute x8, starting transfers between devices, padded_2(): lax.ppermute(head, axis, [((i + 1) % count, i) for i in range(ends)])  26 us
  transfers between devices with their start and end apart: 16, of which 3 were waited for; matrix products, arithmetic and copies ran while one was open for 0% of the time, Pallas kernels for 0%

profile of v1, /device:TPU:1, one launch (start us, length us, event | category | flops | bytes accessed | tf_op | source)
XLA Modules:
  0.0 971.2 jit_solution(2014521607667818468)
XLA Ops:
  0.6 1.5 multiply_reduce_fusion.5
  2.1 106.1 %psum.70 = f32[]{:T(128)} all-reduce(f32[]{:T(128)} %multiply_reduce_fusion.5), channel_id=1, replica_groups=mesh['tor'=8,'pol'=64] {'tor','pol'}, use_global_device_ids=true, to_apply=%region_1.0 | all-reduce | flops 1 | bytes 8 | tf_op jit(solution)/shard_map/psum | solution.py:149
  109.9 2.5 collective-permute-start
  112.4 4.9 collective-permute-start.1
  117.3 1.9 collective-permute-start.2
  119.3 3.0 collective-permute-start.4
  122.3 1.9 collective-permute-start.5
  124.3 4.5 collective-permute-start.6
  128.9 1.9 collective-permute-start.7
  130.9 5.8 collective-permute-start.3
  139.1 138.6 %psum.71 = f32[1]{0:T(128)} all-reduce(f32[1]{0:T(128)} %bitcast.16), channel_id=1, replica_groups=mesh['tor'=8,'pol'=64] {'pol'}, use_global_device_ids=true, to_apply=%region_6.7 | all-reduce | flops 1 | bytes 8 | tf_op jit(solution)/shard_map/psum | solution.py:174
  277.8 17.2 %psum.72 = f32[]{:T(128)} all-reduce(f32[]{:T(128)} %bitcast.17), channel_id=1, replica_groups=mesh['tor'=8,'pol'=64] {'tor'}, use_global_device_ids=true, to_apply=%region_7.8 | all-reduce | flops 1 | bytes 8 | tf_op jit(solution)/shard_map/psum | solution.py:175
  296.2 106.4 %psum.73 = f32[]{:T(128)} all-reduce(f32[]{:T(128)} %multiply_reduce_fusion.4), channel_id=1, replica_groups=mesh['tor'=8,'pol'=64] {'tor','pol'}, use_global_device_ids=true, to_apply=%region_9.10 | all-reduce | flops 1 | bytes 8 | tf_op jit(solution)/shard_map/psum | solution.py:182
  404.1 3.7 collective-permute-start.8
  407.8 3.7 collective-permute-start.9
  411.6 4.1 collective-permute-start.10
  415.7 1.9 collective-permute-start.11
  419.7 1.8 collective-permute-done.11
  422.6 1.4 pad_maximum_fusion.10
  424.0 135.0 %psum.74 = f32[2]{0:T(128)S(1)} all-reduce(f32[2]{0:T(128)S(1)} %pad_maximum_fusion.10), channel_id=1, replica_groups=mesh['tor'=8,'pol'=64] {'pol'}, use_global_device_ids=true, to_apply=%region_15.16 | all-reduce | flops 2 | bytes 16 | tf_op jit(solution)/shard_map/psum | solution.py:174
  559.0 12.5 %psum.75 = f32[2]{0:T(128)S(1)} all-reduce(f32[2]{0:T(128)S(1)} %psum.74), channel_id=1, replica_groups=mesh['tor'=8,'pol'=64] {'tor'}, use_global_device_ids=true, to_apply=%region_16.17 | all-reduce | flops 2 | bytes 16 | tf_op jit(solution)/shard_map/psum | solution.py:175
  572.1 1.9 multiply_reduce_fusion.2
  574.0 108.6 %psum.76 = f32[]{:T(128)} all-reduce(f32[]{:T(128)} %multiply_reduce_fusion.2), channel_id=1, replica_groups=mesh['tor'=8,'pol'=64] {'tor','pol'}, use_global_device_ids=true, to_apply=%region_18.19 | all-reduce | flops 1 | bytes 8 | tf_op jit(solution)/shard_map/psum | solution.py:182
  684.5 3.5 collective-permute-start.12
  688.0 3.9 collective-permute-start.13
  692.0 4.1 collective-permute-start.14
  696.1 1.9 collective-permute-start.15
  703.1 2.0 pad_maximum_fusion.11
  705.1 136.2 %psum.77 = f32[3]{0:T(128)S(1)} all-reduce(f32[3]{0:T(128)S(1)} %pad_maximum_fusion.11), channel_id=1, replica_groups=mesh['tor'=8,'pol'=64] {'pol'}, use_global_device_ids=true, to_apply=%region_25.26 | all-reduce | flops 3 | bytes 24 | tf_op jit(solution)/shard_map/psum | solution.py:174
  841.3 12.5 %psum.78 = f32[3]{0:T(128)S(1)} all-reduce(f32[3]{0:T(128)S(1)} %psum.77), channel_id=1, replica_groups=mesh['tor'=8,'pol'=64] {'tor'}, use_global_device_ids=true, to_apply=%region_26.27 | all-reduce | flops 3 | bytes 24 | tf_op jit(solution)/shard_map/psum | solution.py:175
  856.9 2.6 fusion.13
  860.2 108.1 %psum.79 = f32[]{:T(128)} all-reduce(f32[]{:T(128)} %fusion.13), channel_id=1, replica_groups=mesh['tor'=8,'pol'=64] {'tor','pol'}, use_global_device_ids=true, to_apply=%region_28.29 | all-reduce | flops 1 | bytes 8 | tf_op jit(solution)/shard_map/psum | solution.py:182
  (117 shorter events, 12.4 us)
Async XLA Ops:
  0.6 108.3 %copy-start.2 = (f32[6,1,8,256]{3,2,1,0:T(8,128)S(1)}, f32[6,1,8,256]{3,2,1,0:T(8,128)}, u32[]{:S(2)}) copy-start(f32[6,1,8,256]{3,2,1,0:T(8,128)} %param.5) | copy-start | bytes 147460
  108.9 8.4 copy-start
  109.9 26.9 %collective-permute-start = (bf16[6,1,8,256]{3,2,1,0:T(8,128)(2,1)S(1)}, bf16[6,1,8,256]{3,2,1,0:T(8,128)(2,1)S(1)}, u32[]{:S(2)}, u32[]{:S(2)}) collective-permute-start(bf16[6,1,8,256]{3,2,1,0:T(8,128)(2,1)S(1)} %get-tuple-element.17), channel_id=1, source_target_pairs={{0,64},{64,128},{128,192},{192,256},{256,320},{320,384},{384,448},... | collective-permute-start | bytes 73736 | tf_op jit(solution)/shard_map/ppermute | solution.py:20
  112.4 24.4 %collective-permute-start.1 = (bf16[6,1,8,256]{3,2,1,0:T(8,128)(2,1)S(1)}, bf16[6,1,8,256]{3,2,1,0:T(8,128)(2,1)S(1)}, u32[]{:S(2)}, u32[]{:S(2)}) collective-permute-start(bf16[6,1,8,256]{3,2,1,0:T(8,128)(2,1)S(1)} %get-tuple-element.17), channel_id=1, source_target_pairs={{64,0},{128,64},{192,128},{256,192},{320,256},{384,320},{448,384},... | collective-permute-start | bytes 73736 | tf_op jit(solution)/shard_map/ppermute | solution.py:22
  117.3 19.5 %collective-permute-start.2 = (bf16[6,1,8,256]{3,2,1,0:T(8,128)(2,1)S(1)}, bf16[6,1,8,256]{3,2,1,0:T(8,128)(2,1)S(1)}, u32[]{:S(2)}, u32[]{:S(2)}) collective-permute-start(bf16[6,1,8,256]{3,2,1,0:T(8,128)(2,1)S(1)} %convert_element_type.95), channel_id=1, source_target_pairs={{0,64},{64,128},{128,192},{192,256},{256,320},{320,384},{384,448},... | collective-permute-start | bytes 73736 | tf_op jit(solution)/shard_map/ppermute | solution.py:20
  119.3 5.1 collective-permute-start.4
  122.3 6.6 collective-permute-start.5
  124.3 6.5 collective-permute-start.6
  128.9 7.7 collective-permute-start.7
  130.9 6.7 collective-permute-start.3
  137.7 0.7 copy-start.3
  139.1 264.9 %copy-start.1 = (f32[6,6,1,8,256]{4,3,2,1,0:T(8,128)S(1)}, f32[6,6,1,8,256]{4,3,2,1,0:T(8,128)}, u32[]{:S(2)}) copy-start(f32[6,6,1,8,256]{4,3,2,1,0:T(8,128)} %param.7) | copy-start | bytes 884740
  404.1 17.6 %collective-permute-start.8 = (bf16[6,1,8,256]{3,2,1,0:T(8,128)(2,1)S(1)}, bf16[6,1,8,256]{3,2,1,0:T(8,128)(2,1)S(1)}, u32[]{:S(2)}, u32[]{:S(2)}) collective-permute-start(bf16[6,1,8,256]{3,2,1,0:T(8,128)(2,1)S(1)} %get-tuple-element.11), channel_id=1, source_target_pairs={{0,64},{64,128},{128,192},{192,256},{256,320},{320,384},{384,448},... | collective-permute-start | bytes 73736 | tf_op jit(solution)/shard_map/ppermute | solution.py:20
  407.8 13.9 %collective-permute-start.9 = (bf16[6,1,8,256]{3,2,1,0:T(8,128)(2,1)S(1)}, bf16[6,1,8,256]{3,2,1,0:T(8,128)(2,1)S(1)}, u32[]{:S(2)}, u32[]{:S(2)}) collective-permute-start(bf16[6,1,8,256]{3,2,1,0:T(8,128)(2,1)S(1)} %get-tuple-element.11), channel_id=1, source_target_pairs={{64,0},{128,64},{192,128},{256,192},{320,256},{384,320},{448,384},... | collective-permute-start | bytes 73736 | tf_op jit(solution)/shard_map/ppermute | solution.py:22
  411.6 8.2 collective-permute-start.10
  415.7 5.8 collective-permute-start.11
  684.5 17.6 %collective-permute-start.12 = (bf16[6,1,8,256]{3,2,1,0:T(8,128)(2,1)S(1)}, bf16[6,1,8,256]{3,2,1,0:T(8,128)(2,1)S(1)}, u32[]{:S(2)}, u32[]{:S(2)}) collective-permute-start(bf16[6,1,8,256]{3,2,1,0:T(8,128)(2,1)S(1)} %get-tuple-element.8), channel_id=1, source_target_pairs={{0,64},{64,128},{128,192},{192,256},{256,320},{320,384},{384,448},... | collective-permute-start | bytes 73736 | tf_op jit(solution)/shard_map/ppermute | solution.py:20
  688.0 14.1 %collective-permute-start.13 = (bf16[6,1,8,256]{3,2,1,0:T(8,128)(2,1)S(1)}, bf16[6,1,8,256]{3,2,1,0:T(8,128)(2,1)S(1)}, u32[]{:S(2)}, u32[]{:S(2)}) collective-permute-start(bf16[6,1,8,256]{3,2,1,0:T(8,128)(2,1)S(1)} %get-tuple-element.8), channel_id=1, source_target_pairs={{64,0},{128,64},{192,128},{256,192},{320,256},{384,320},{448,384},... | collective-permute-start | bytes 73736 | tf_op jit(solution)/shard_map/ppermute | solution.py:22
  692.0 8.9 collective-permute-start.14
  696.1 5.8 collective-permute-start.15
